TPU v7x, 32 devices: a whole 2x2x4 slice. The times are simulated.
32 devices in a mesh: band: 2 (over x), img: 4 (over z), fsdp: 4 (over y, core).
Axes of the slice: x: 2, y: 2, z: 4, core: 2. Of those that a mesh axis runs over, the one named last changes fastest.
Arguments:
- block_input: bfloat16 [384, 14, 14, 512], P(('img', 'fsdp'), 'band'), may hold values from -6 to 6
- slot_used: int32 [16, 24], P(('img', 'fsdp')), may hold values from 0 to 1, as said below
- cotangent: bfloat16 [384, 14, 14, 512], P(('img', 'fsdp'), 'band'), may hold values from -6 to 6
- ln1_gain: bfloat16 [512], P('fsdp'), may hold values from 0.25 to 1.75
- ln1_bias: bfloat16 [512], P('fsdp'), may hold values from -3 to 3
- w_qkv: bfloat16 [512, 1536], P('fsdp')
- q_bias: bfloat16 [512], P('fsdp'), may hold values from -3 to 3
- v_bias: bfloat16 [512], P('fsdp'), may hold values from -3 to 3
- rel_table: bfloat16 [16, 169], P('fsdp'), may hold values from -4 to 4
- w_out: bfloat16 [512, 512], P('fsdp'), may hold values from -0.75 to 0.75
- out_bias: bfloat16 [512], P('fsdp'), may hold values from -3 to 3
- ln2_gain: bfloat16 [512], P('fsdp'), may hold values from 0.25 to 1.75
- ln2_bias: bfloat16 [512], P('fsdp'), may hold values from -3 to 3
- w_fc1: bfloat16 [512, 2048], P('fsdp'), may hold values from -0.25 to 0.25
- fc1_bias: bfloat16 [2048], P('fsdp'), may hold values from -3 to 3
- w_fc2: bfloat16 [2048, 512], P('fsdp'), may hold values from -0.125 to 0.125
- fc2_bias: bfloat16 [512], P('fsdp'), may hold values from -3 to 3
Outputs:
- block_output: bfloat16 [384, 14, 14, 512], P(('img', 'fsdp'), 'band')
- input_grad: float32 [384, 14, 14, 512], P(('img', 'fsdp'), 'band')
- ln1_gain_grad: float32 [512], P('fsdp')
- ln1_bias_grad: float32 [512], P('fsdp')
- w_qkv_grad: float32 [512, 1536], P('fsdp')
- q_bias_grad: float32 [512], P('fsdp')
- v_bias_grad: float32 [512], P('fsdp')
- rel_table_grad: float32 [16, 169], P('fsdp')
- w_out_grad: float32 [512, 512], P('fsdp')
- out_bias_grad: float32 [512], P('fsdp')
- ln2_gain_grad: float32 [512], P('fsdp')
- ln2_bias_grad: float32 [512], P('fsdp')
- w_fc1_grad: float32 [512, 2048], P('fsdp')
- fc1_bias_grad: float32 [2048], P('fsdp')
- w_fc2_grad: float32 [2048, 512], P('fsdp')
- fc2_bias_grad: float32 [512], P('fsdp')
Inputs may be any that keep to these rules, and one draw needn't show every extreme that they name: `slot_used`: each row holds between 16 and 24 ones in any positions; both counts occur in every draw.
All inputs are finite; a program needn't handle non-finite values.
Results may differ from a plain program's by a relative error of at most 0.013.
The roundings to bfloat16 on the way count: a program that leaves them out, or rounds other values in their place, can miss the bound.
Values may be sent and summed in bfloat16 or wider, within the bound.
No kernel may reach another device: no remote copies, remote signals or barrier semaphores. Data moves between devices by JAX's collectives and lax.ppermute only.
A program may use at most 320 MiB of HBM per device.

v0:
```python
import jax
import jax.numpy as jnp
from jax import lax
from jax.sharding import PartitionSpec as P

D = 512
HEADS = 16
WIN = 7
SHIFT = 3
SIDE = 14
TABLE = 169
EPSILON = 1e-05
NEGATIVE = -1e30


def from_partner(value, axis, apart):
    mask = 2**apart
    pairs = [(source, source ^ mask) for source in range(lax.axis_size(axis))]
    return lax.ppermute(value, axis, pairs)


def rel_onehot():
    length = WIN * WIN
    places = jnp.arange(length)
    rowpos = places // WIN
    colpos = places % WIN
    index = (rowpos[:, None] - rowpos[None, :] + WIN - 1) * (2 * WIN - 1) + (
        colpos[:, None] - colpos[None, :] + WIN - 1
    )
    return (index.reshape(-1)[:, None] == jnp.arange(TABLE)[None, :]).astype(jnp.float32)


def window_same():
    cells = jnp.arange(SIDE)
    region = jnp.where(cells < SIDE - WIN, 0, jnp.where(cells < SIDE - SHIFT, 1, 2))
    label = region[:, None] * 3 + region[None, :]
    per_image = SIDE // WIN
    label = (
        label.reshape(per_image, WIN, per_image, WIN).transpose(0, 2, 1, 3).reshape(-1, WIN * WIN)
    )
    return label[:, :, None] == label[:, None, :]


def normalize(values):
    center = values - jnp.mean(values, -1, keepdims=True)
    spread = jnp.mean(center * center, -1, keepdims=True)
    rstd = lax.rsqrt(spread + EPSILON)
    return (center * rstd, rstd)


def norm_back(grad_hat, normal, rstd):
    return rstd * (
        grad_hat
        - jnp.mean(grad_hat, -1, keepdims=True)
        - normal * jnp.mean(grad_hat * normal, -1, keepdims=True)
    )


def gelu_slope(pre):
    return (
        0.5 * (1.0 + lax.erf(pre * 0.7071067811865476))
        + pre * jnp.exp(-0.5 * pre * pre) * 0.3989422804014327
    )


def to_windows(tensor):
    count = tensor.shape[0]
    width = tensor.shape[-1]
    return (
        tensor.reshape(count, WIN, SIDE // WIN, WIN, width)
        .transpose(0, 2, 1, 3, 4)
        .reshape(-1, width)
    )


def from_windows(tensor, count):
    width = tensor.shape[-1]
    return (
        tensor.reshape(count, SIDE // WIN, WIN, WIN, width)
        .transpose(0, 2, 1, 3, 4)
        .reshape(count, WIN, SIDE, width)
    )


def attention_logits(queries, keys_win, bias, same):
    scores = jnp.einsum("wqhd,wkhd->whqk", queries, keys_win, preferred_element_type=jnp.float32)
    length = scores.shape[-1]
    scores = scores.reshape(-1, same.shape[0], HEADS, length, length) + bias[None, None]
    scores = jnp.where(same[None, :, None], scores, NEGATIVE)
    return scores.reshape(-1, HEADS, length, length)


def shards(
    block_input,
    slot_used,
    cotangent,
    ln1_gain,
    ln1_bias,
    w_qkv,
    q_bias,
    v_bias,
    rel_table,
    w_out,
    out_bias,
    ln2_gain,
    ln2_bias,
    w_fc1,
    fc1_bias,
    w_fc2,
    fc2_bias,
):
    f32 = jnp.float32
    bf16 = jnp.bfloat16
    (
        gain_low,
        beta_low,
        weight_qkv,
        qbias_low,
        vbias_low,
        table,
        weight_out,
        pbias_low,
        gain2_low,
        beta2_low,
        weight_up,
        ubias_low,
        weight_down,
        dbias_low,
    ) = (
        lax.all_gather(ln1_gain, "fsdp", axis=0, tiled=True),
        lax.all_gather(ln1_bias, "fsdp", axis=0, tiled=True),
        lax.all_gather(w_qkv, "fsdp", axis=0, tiled=True),
        lax.all_gather(q_bias, "fsdp", axis=0, tiled=True),
        lax.all_gather(v_bias, "fsdp", axis=0, tiled=True),
        lax.all_gather(rel_table, "fsdp", axis=0, tiled=True),
        lax.all_gather(w_out, "fsdp", axis=0, tiled=True),
        lax.all_gather(out_bias, "fsdp", axis=0, tiled=True),
        lax.all_gather(ln2_gain, "fsdp", axis=0, tiled=True),
        lax.all_gather(ln2_bias, "fsdp", axis=0, tiled=True),
        lax.all_gather(w_fc1, "fsdp", axis=0, tiled=True),
        lax.all_gather(fc1_bias, "fsdp", axis=0, tiled=True),
        lax.all_gather(w_fc2, "fsdp", axis=0, tiled=True),
        lax.all_gather(fc2_bias, "fsdp", axis=0, tiled=True),
    )
    gain_one = gain_low.astype(f32)
    beta_one = beta_low.astype(f32)
    query_bias = qbias_low.astype(f32)
    value_bias = vbias_low.astype(f32)
    proj_bias = pbias_low.astype(f32)
    gain_two = gain2_low.astype(f32)
    beta_two = beta2_low.astype(f32)
    up_bias = ubias_low.astype(f32)
    down_bias = dbias_low.astype(f32)
    slots = block_input.shape[0]
    length = WIN * WIN
    head_dim = D // HEADS
    scale = head_dim ** (-0.5)
    per_image = SIDE // WIN
    onehot = rel_onehot()
    bias = jnp.dot(table.astype(f32), onehot.T, precision=lax.Precision.HIGHEST).reshape(
        HEADS, length, length
    )
    same = lax.dynamic_slice_in_dim(window_same(), lax.axis_index("band") * per_image, per_image, 0)
    inputs = block_input.astype(f32).reshape(-1, D)
    hat_one, rstd_one = normalize(inputs)
    normed = (hat_one * gain_one + beta_one).astype(bf16).reshape(slots, WIN, SIDE, D)
    arrived = from_partner(normed[:, :SHIFT], "band", 0)
    shifted = jnp.roll(jnp.concatenate([normed[:, SHIFT:], arrived], axis=1), -SHIFT, axis=2)
    windows = to_windows(shifted)
    qkv = jnp.dot(windows, weight_qkv, preferred_element_type=f32)
    queries = ((qkv[:, :D] + query_bias) * scale).astype(bf16).reshape(-1, length, HEADS, head_dim)
    keys_win = qkv[:, D : 2 * D].astype(bf16).reshape(-1, length, HEADS, head_dim)
    values = (qkv[:, 2 * D :] + value_bias).astype(bf16).reshape(-1, length, HEADS, head_dim)
    scores = attention_logits(queries, keys_win, bias, same)
    peak = jnp.max(scores, -1, keepdims=True)
    lse = peak + jnp.log(jnp.sum(jnp.exp(scores - peak), -1, keepdims=True))
    probs = jnp.exp(scores - lse).astype(bf16)
    attended = (
        jnp.einsum("whqk,wkhd->wqhd", probs, values, preferred_element_type=f32)
        .astype(bf16)
        .reshape(-1, D)
    )
    proj = (jnp.dot(attended, weight_out, preferred_element_type=f32) + proj_bias).astype(bf16)
    framed = jnp.roll(from_windows(proj, slots), SHIFT, axis=2)
    returned = from_partner(framed[:, WIN - SHIFT :], "band", 0)
    restored = jnp.concatenate([returned, framed[:, : WIN - SHIFT]], axis=1)
    resid = inputs + restored.astype(f32).reshape(-1, D)
    hat_two, rstd_two = normalize(resid)
    normed_two = (hat_two * gain_two + beta_two).astype(bf16)
    pre = jnp.dot(normed_two, weight_up, preferred_element_type=f32) + up_bias
    act = jax.nn.gelu(pre, approximate=False).astype(bf16)
    mlp_out = jnp.dot(act, weight_down, preferred_element_type=f32) + down_bias
    used_rows = jnp.repeat(slot_used.reshape(-1).astype(f32), WIN * SIDE)[:, None]
    output = (used_rows * (resid + mlp_out)).astype(bf16)
    grad_out = cotangent.astype(f32).reshape(-1, D) * used_rows
    grad_low = grad_out.astype(bf16)
    grad_down = jnp.dot(act.T, grad_low, preferred_element_type=f32)
    grad_downb = jnp.sum(grad_out, 0)
    grad_pre = jnp.dot(grad_low, weight_down.T, preferred_element_type=f32) * gelu_slope(pre)
    grad_upb = jnp.sum(grad_pre, 0)
    grad_hidden = grad_pre.astype(bf16)
    grad_up = jnp.dot(normed_two.T, grad_hidden, preferred_element_type=f32)
    grad_normed_two = jnp.dot(grad_hidden, weight_up.T, preferred_element_type=f32)
    grad_gain_two = jnp.sum(grad_normed_two * hat_two, 0)
    grad_beta_two = jnp.sum(grad_normed_two, 0)
    grad_resid = grad_out + norm_back(grad_normed_two * gain_two, hat_two, rstd_two)
    grad_projb = jnp.sum(grad_resid, 0)
    resid_low = grad_resid.astype(bf16).reshape(slots, WIN, SIDE, D)
    crossed = from_partner(resid_low[:, :SHIFT], "band", 0)
    grad_proj = to_windows(
        jnp.roll(jnp.concatenate([resid_low[:, SHIFT:], crossed], axis=1), -SHIFT, axis=2)
    )
    grad_wout = jnp.dot(attended.T, grad_proj, preferred_element_type=f32)
    grad_attended = (
        jnp.dot(grad_proj, weight_out.T, preferred_element_type=f32)
        .astype(bf16)
        .reshape(-1, length, HEADS, head_dim)
    )
    recomputed = jnp.exp(attention_logits(queries, keys_win, bias, same) - lse)
    grad_probs = jnp.einsum("wqhd,wkhd->whqk", grad_attended, values, preferred_element_type=f32)
    grad_scores = recomputed * (grad_probs - jnp.sum(recomputed * grad_probs, -1, keepdims=True))
    grad_table = jnp.dot(
        jnp.sum(grad_scores, 0).reshape(HEADS, length * length),
        onehot,
        precision=lax.Precision.HIGHEST,
    )
    grad_logits = grad_scores.astype(bf16)
    grad_queries = (
        jnp.einsum("whqk,wkhd->wqhd", grad_logits, keys_win, preferred_element_type=f32).reshape(
            -1, D
        )
        * scale
    )
    grad_keys = jnp.einsum(
        "whqk,wqhd->wkhd", grad_logits, queries, preferred_element_type=f32
    ).reshape(-1, D)
    grad_values = jnp.einsum(
        "whqk,wqhd->wkhd", probs, grad_attended, preferred_element_type=f32
    ).reshape(-1, D)
    grad_qbias = jnp.sum(grad_queries, 0)
    grad_vbias = jnp.sum(grad_values, 0)
    grad_qkv = jnp.concatenate([grad_queries, grad_keys, grad_values], axis=1).astype(bf16)
    grad_wqkv = jnp.dot(windows.T, grad_qkv, preferred_element_type=f32)
    grad_shifted = jnp.dot(grad_qkv, weight_qkv.T, preferred_element_type=f32).astype(bf16)
    grad_framed = jnp.roll(from_windows(grad_shifted, slots), SHIFT, axis=2)
    grad_back = from_partner(grad_framed[:, WIN - SHIFT :], "band", 0)
    grad_normed = (
        jnp.concatenate([grad_back, grad_framed[:, : WIN - SHIFT]], axis=1)
        .astype(f32)
        .reshape(-1, D)
    )
    grad_gain_one = jnp.sum(grad_normed * hat_one, 0)
    grad_beta_one = jnp.sum(grad_normed, 0)
    grad_input = grad_resid + norm_back(grad_normed * gain_one, hat_one, rstd_one)
    final_output = output.reshape(slots, WIN, SIDE, D)
    final_grad = grad_input.reshape(slots, WIN, SIDE, D)
    s01, s02, s03, s04, s05, s06, s07, s08, s09, s10, s11, s12, s13, s14 = lax.psum(
        (
            grad_gain_one,
            grad_beta_one,
            grad_wqkv,
            grad_qbias,
            grad_vbias,
            grad_table,
            grad_wout,
            grad_projb,
            grad_gain_two,
            grad_beta_two,
            grad_up,
            grad_upb,
            grad_down,
            grad_downb,
        ),
        ("band", "img"),
    )
    r01, r02, r03, r04, r05, r06, r07, r08, r09, r10, r11, r12, r13, r14 = (
        lax.psum_scatter(s01, "fsdp", scatter_dimension=0, tiled=True),
        lax.psum_scatter(s02, "fsdp", scatter_dimension=0, tiled=True),
        lax.psum_scatter(s03, "fsdp", scatter_dimension=0, tiled=True),
        lax.psum_scatter(s04, "fsdp", scatter_dimension=0, tiled=True),
        lax.psum_scatter(s05, "fsdp", scatter_dimension=0, tiled=True),
        lax.psum_scatter(s06, "fsdp", scatter_dimension=0, tiled=True),
        lax.psum_scatter(s07, "fsdp", scatter_dimension=0, tiled=True),
        lax.psum_scatter(s08, "fsdp", scatter_dimension=0, tiled=True),
        lax.psum_scatter(s09, "fsdp", scatter_dimension=0, tiled=True),
        lax.psum_scatter(s10, "fsdp", scatter_dimension=0, tiled=True),
        lax.psum_scatter(s11, "fsdp", scatter_dimension=0, tiled=True),
        lax.psum_scatter(s12, "fsdp", scatter_dimension=0, tiled=True),
        lax.psum_scatter(s13, "fsdp", scatter_dimension=0, tiled=True),
        lax.psum_scatter(s14, "fsdp", scatter_dimension=0, tiled=True),
    )
    return (
        final_output,
        final_grad,
        r01,
        r02,
        r03,
        r04,
        r05,
        r06,
        r07,
        r08,
        r09,
        r10,
        r11,
        r12,
        r13,
        r14,
    )


def solution(mesh):
    placed = (
        P(("img", "fsdp"), "band", None, None),
        P(("img", "fsdp"), None),
        P(("img", "fsdp"), "band", None, None),
        P("fsdp"),
        P("fsdp"),
        P("fsdp", None),
        P("fsdp"),
        P("fsdp"),
        P("fsdp", None),
        P("fsdp", None),
        P("fsdp"),
        P("fsdp"),
        P("fsdp"),
        P("fsdp", None),
        P("fsdp"),
        P("fsdp", None),
        P("fsdp"),
    )
    return jax.shard_map(
        shards,
        mesh=mesh,
        in_specs=placed,
        out_specs=(
            P(("img", "fsdp"), "band", None, None),
            P(("img", "fsdp"), "band", None, None),
            P("fsdp"),
            P("fsdp"),
            P("fsdp", None),
            P("fsdp"),
            P("fsdp"),
            P("fsdp", None),
            P("fsdp", None),
            P("fsdp"),
            P("fsdp"),
            P("fsdp"),
            P("fsdp", None),
            P("fsdp"),
            P("fsdp", None),
            P("fsdp"),
        ),
        check_vma=False,
    )
```

profile of v0, /device:TPU:0, one launch (start us, length us, event | category | flops | bytes accessed | tf_op | source)
XLA Modules:
  0.0 890.9 jit_solution(15372807008228085413)
XLA Ops:
  8.0 6.2 all-gather
  14.2 5.4 all-gather.1
  32.7 5.0 all-gather.3
  37.7 5.0 all-gather.2
  42.8 5.2 all-gather.5
  48.0 5.4 all-gather.4
  54.8 7.9 all_gather.48
  68.0 5.2 reshape.401
  73.1 6.2 fusion.53
  84.7 11.5 %reshape.462 = bf16[48,49,16,32]{3,2,1,0:T(8,128)(2,1)} reshape(bf16[2352,512]{1,0:T(8,128)(2,1)} %get-tuple-element.117) | data formatting | bytes 4816896 | tf_op jit(solution)/shard_map/reshape | solution.py:171
  96.2 13.5 %copy.127 = bf16[48,49,16,32]{1,3,2,0:T(8,128)(2,1)} copy(bf16[48,49,16,32]{3,2,1,0:T(8,128)(2,1)} %reshape.462) | data formatting | bytes 4816896 | tf_op jit(solution)/shard_map/reshape | solution.py:171
  109.8 11.5 %reshape.463 = bf16[48,49,16,32]{3,2,1,0:T(8,128)(2,1)} reshape(bf16[2352,512]{1,0:T(8,128)(2,1)} %slice.113) | data formatting | bytes 4816896 | tf_op jit(solution)/shard_map/reshape | solution.py:172
  121.3 13.5 %copy.128 = bf16[48,49,16,32]{1,3,2,0:T(8,128)(2,1)} copy(bf16[48,49,16,32]{3,2,1,0:T(8,128)(2,1)} %reshape.463) | data formatting | bytes 4816896 | tf_op jit(solution)/shard_map/reshape | solution.py:172
  134.9 13.4 %fusion.15 = (f32[48,16,49]{2,1,0:T(8,128)S(1)}, f32[48,16,49,49]{2,3,1,0:T(8,128)}) fusion(f32[16,49,49]{1,2,0:T(8,128)S(1)} %copy.129, pred[48,49,49]{1,2,0:T(8,128)(4,1)S(1)} %bitcast.95, bf16[48,49,16,32]{1,3,2,0:T(8,128)(2,1)} %copy.127, bf16[48,49,16,32]{1,3,2,0:T(8,128)(2,1)} %copy.128), kind=kOutput, calls=%fused_computation.30 | convolution fusion | flops 123508224 | bytes 12612208 | tf_op jit(solution)/shard_map/wqhd,wkhd->whqk/dot_general | solution.py:86
  148.3 13.4 %exponential_reduce_fusion = f32[48,16,49]{2,1,0:T(8,128)S(1)} fusion(f32[48,16,49,49]{2,3,1,0:T(8,128)} %get-tuple-element.122, f32[48,16,49]{2,1,0:T(8,128)S(1)} %get-tuple-element.121, f32[16,49,49]{1,2,0:T(8,128)S(1)} %copy.129, pred[48,49,49]{1,2,0:T(8,128)(4,1)S(1)} %bitcast.96), kind=kLoop, calls=%fused_computation.5 | loop fusion | flops 7338240 | bytes 7945840 | tf_op jit(solution)/shard_map/reduce_sum | solution.py:176
  162.5 11.5 %reshape.461 = bf16[48,49,16,32]{3,2,1,0:T(8,128)(2,1)} reshape(bf16[2352,512]{1,0:T(8,128)(2,1)} %get-tuple-element.118) | data formatting | bytes 4816896 | tf_op jit(solution)/shard_map/reshape | solution.py:173
  174.0 13.5 %copy.130 = bf16[48,49,16,32]{1,3,2,0:T(8,128)(2,1)} copy(bf16[48,49,16,32]{3,2,1,0:T(8,128)(2,1)} %reshape.461) | data formatting | bytes 4816896 | tf_op jit(solution)/shard_map/reshape | solution.py:173
  187.6 14.4 %convert_bitcast_fusion.1 = bf16[48,49,16,32]{1,3,2,0:T(8,128)(2,1)} fusion(bf16[48,49,16,32]{1,3,2,0:T(8,128)(2,1)} %copy.130, f32[48,16,49,49]{2,3,1,0:T(8,128)} %get-tuple-element.122, f32[48,16,49]{2,1,0:T(8,128)} %log_add_fusion, f32[16,49,49]{1,2,0:T(8,128)S(1)} %copy.129, pred[48,49,49]{1,2,0:T(8,128)(4,1)S(1)} %bitcast.97), kind=kOutput, calls=%fused_computation.38 | convolution fusion | flops 126594048 | bytes 12612208 | tf_op jit(solution)/shard_map/whqk,wkhd->wqhd/dot_general | solution.py:179
  201.9 9.5 %copy.132 = bf16[48,49,16,32]{1,0,3,2:T(8,128)(2,1)} copy(bf16[48,49,16,32]{1,3,2,0:T(8,128)(2,1)} %convert_bitcast_fusion.1) | data formatting | bytes 4816896 | tf_op jit(solution)/shard_map/convert_element_type | solution.py:180
  211.5 9.2 %reshape.405 = bf16[2352,512]{0,1:T(8,128)(2,1)} reshape(bf16[48,49,16,32]{1,0,3,2:T(8,128)(2,1)} %copy.132) | data formatting | bytes 4816896 | tf_op jit(solution)/shard_map/reshape | solution.py:181
  225.2 5.1 reshape.406
  240.0 5.0 all-gather.6
  245.1 5.1 all-gather.7
  250.1 5.4 all-gather.8
  261.2 6.3 reshape.409
  267.6 6.3 reshape.399
  281.2 5.3 copy.134
  286.5 6.4 reshape.420
  292.9 7.1 add.283
  300.0 49.9 %fusion.2 = (bf16[2352,2048]{1,0:T(8,128)(2,1)}, f32[2352,2048]{1,0:T(8,128)}) fusion(f32[2048]{0:T(1024)S(1)} %bitcast.122, bf16[512,2048]{1,0:T(8,128)(2,1)} %all-gather.16.cloned.1.call-done, f32[2352,512]{1,0:T(8,128)} %add.283, f32[512]{0:T(512)S(1)} %bitcast.125, f32[512]{0:T(512)S(1)} %bitcast.115, f32[2352]{0:T(1024)S(1)} %rsqrt.25, f32[2352]{0:T(1024)S(1)} %div.52), kind=kOutput, calls=%fused_computation.9 | convolution fusion | flops 5256437760 | bytes 35846528 | tf_op jit(solution)/shard_map/dot_general | solution.py:190
  349.9 18.1 %fusion.50 = (f32[2048]{0:T(1024)}, bf16[2352,2048]{1,0:T(8,128)(2,1)}) fusion(f32[2352,2048]{1,0:T(8,128)} %get-tuple-element.124, f32[2048]{0:T(1024)S(1)} %bitcast.123, bf16[2048,512]{1,0:T(8,128)(2,1)} %all-gather.18.cloned.1.call-done, f32[2352,512]{1,0:T(8,128)} %reshape.409, f32[2352]{0:T(1024)S(1)} %copy-done.31), kind=kOutput, calls=%fused_computation.130 | convolution fusion | flops 4992710656 | bytes 35841216 | tf_op jit(solution)/shard_map/dot_general | solution.py:199
  368.0 12.3 %multiply_reduce_fusion.3 = (f32[512]{0:T(512)}, f32[2352]{0:T(1024)S(1)}, f32[2352]{0:T(1024)S(1)}, f32[512]{0:T(512)}, f32[2352,512]{1,0:T(8,128)S(1)}) fusion(f32[2352,512]{1,0:T(8,128)S(1)} %copy-done.9, f32[2352]{0:T(1024)S(1)} %rsqrt.25, f32[2352]{0:T(1024)S(1)} %div.52, f32[512]{0:T(512)S(1)} %bitcast.116, bf16[512,2048]{1,0:T(8,128)(2,1)S(1)} %copy-done.56, ...), kind=kOutput, calls=%fused_computation.51 | convolution fusion | flops 4943333376 | bytes 21408512 | tf_op jit(solution)/shard_map/dot_general | solution.py:203
  393.5 23.3 %collective-permute-done.2 = bf16[24,3,14,512]{3,0,2,1:T(8,128)(2,1)S(1)} collective-permute-done((bf16[24,3,14,512]{3,0,2,1:T(8,128)(2,1)S(1)}, bf16[24,3,14,512]{3,0,2,1:T(8,128)(2,1)S(1)}, u32[]{:S(2)}, u32[]{:S(2)}) %collective-permute-start.2) | collective-permute-done | bytes 1032224 | tf_op jit(solution)/shard_map/ppermute | solution.py:19
  423.5 5.1 fusion.55
  431.4 11.5 %reshape.464 = bf16[48,49,16,32]{3,2,1,0:T(8,128)(2,1)} reshape(bf16[2352,512]{1,0:T(8,128)(2,1)} %convolution_convert_fusion.1) | data formatting | bytes 4816896 | tf_op jit(solution)/shard_map/reshape | solution.py:217
  442.9 13.6 %copy.144 = bf16[48,49,16,32]{1,3,2,0:T(8,128)(2,1)} copy(bf16[48,49,16,32]{3,2,1,0:T(8,128)(2,1)} %reshape.464) | data formatting | bytes 4816896 | tf_op jit(solution)/shard_map/reshape | solution.py:217
  456.6 23.3 %multiply_reduce_fusion = (f32[48,16,49]{2,1,0:T(8,128)S(1)}, f32[48,16,49,49]{2,3,1,0:T(8,128)}) fusion(f32[48,16,49,49]{2,3,1,0:T(8,128)} %get-tuple-element.122, f32[48,16,49]{2,1,0:T(8,128)S(1)} %copy-done.8, f32[16,49,49]{1,2,0:T(8,128)S(1)} %copy-done.3, pred[48,49,49]{1,2,0:T(8,128)(4,1)S(1)} %bitcast.98, bf16[48,49,16,32]{1,3,2,0:T(8,128)(2,1)} %copy.144, ...), kind=kOutput, calls=%fused_computation.3 | convolution fusion | flops 127196160 | bytes 20138608 | tf_op jit(solution)/shard_map/wqhd,wkhd->whqk/dot_general | solution.py:220
  479.9 19.4 %bitcast_convert_fusion = (bf16[48,49,16,32]{1,3,2,0:T(8,128)(2,1)}, f32[48,16,32,49]{3,2,1,0:T(8,128)}) fusion(bf16[48,49,16,32]{1,3,2,0:T(8,128)(2,1)} %copy.144, f32[48,16,49,49]{2,3,1,0:T(8,128)} %get-tuple-element.122, f32[48,16,49]{2,1,0:T(8,128)S(1)} %copy-done.8, f32[16,49,49]{1,2,0:T(8,128)S(1)} %copy-done.3, pred[48,49,49]{1,2,0:T(8,128)(4,1)S(1)} %bitcast.99), kind=kOutput, calls=%fused_computation.32 | convolution fusion | flops 126594048 | bytes 17429104 | tf_op jit(solution)/shard_map/whqk,wqhd->wkhd/dot_general | solution.py:237
  499.2 21.2 %fusion.48 = (f32[16,49,49]{1,2,0:T(8,128)}, bf16[48,16,49,49]{2,3,1,0:T(8,128)(2,1)}) fusion(f32[48,16,49,49]{2,3,1,0:T(8,128)} %get-tuple-element.127, f32[48,16,49]{2,1,0:T(8,128)S(1)} %get-tuple-element.126, f32[48,16,49]{2,1,0:T(8,128)S(1)} %copy-done.8, f32[48,16,49,49]{2,3,1,0:T(8,128)} %get-tuple-element.122, f32[16,49,49]{1,2,0:T(8,128)S(1)} %copy-done.3, ...), kind=kLoop, calls=%fused_computation.129 | loop fusion | flops 12869360 | bytes 19163312 | tf_op jit(solution)/shard_map/reduce_sum | solution.py:223
  520.4 10.4 %convert_bitcast_fusion = bf16[48,49,16,32]{1,3,2,0:T(8,128)(2,1)} fusion(bf16[48,49,16,32]{1,3,2,0:T(8,128)(2,1)S(1)} %bitcast.94, bf16[48,16,49,49]{2,3,1,0:T(8,128)(2,1)} %get-tuple-element.115), kind=kOutput, calls=%fused_computation.37 | convolution fusion | flops 119218176 | bytes 8504832 | tf_op jit(solution)/shard_map/whqk,wqhd->wkhd/dot_general | solution.py:234
  530.8 11.9 %multiply_reduce_fusion.1 = (f32[16,32]{1,0:T(8,128)S(1)}, bf16[48,49,16,32]{1,3,2,0:T(8,128)(2,1)}) fusion(bf16[48,49,16,32]{1,3,2,0:T(8,128)(2,1)} %copy.128, bf16[48,16,49,49]{2,3,1,0:T(8,128)(2,1)} %get-tuple-element.115), kind=kOutput, calls=%fused_computation.33 | convolution fusion | flops 121626112 | bytes 8506880 | tf_op jit(solution)/shard_map/whqk,wkhd->wqhd/dot_general | solution.py:229
  542.8 9.6 %copy.151 = bf16[48,49,16,32]{1,0,3,2:T(8,128)(2,1)} copy(bf16[48,49,16,32]{1,3,2,0:T(8,128)(2,1)} %convert_bitcast_fusion) | data formatting | bytes 4816896 | tf_op jit(solution)/shard_map/whqk,wqhd->wkhd/transpose | solution.py:234
  552.3 8.5 reshape.414
  560.8 9.6 %copy.154 = bf16[48,49,16,32]{1,0,3,2:T(8,128)(2,1)} copy(bf16[48,49,16,32]{1,3,2,0:T(8,128)(2,1)} %get-tuple-element.128) | data formatting | bytes 4816896 | tf_op jit(solution)/shard_map/convert.5
  570.4 9.2 %reshape.415 = bf16[2352,512]{0,1:T(8,128)(2,1)} reshape(bf16[48,49,16,32]{1,0,3,2:T(8,128)(2,1)} %copy.154) | data formatting | bytes 4816896 | tf_op jit(solution)/shard_map/reshape | solution.py:239
  579.6 9.4 %copy.148 = bf16[48,49,16,32]{1,0,3,2:T(8,128)(2,1)} copy(bf16[48,49,16,32]{1,3,2,0:T(8,128)(2,1)} %get-tuple-element.120) | data formatting | bytes 4816896 | tf_op jit(solution)/shard_map/mul | solution.py:229
  589.0 9.3 %mul.250 = bf16[2352,512]{0,1:T(8,128)(2,1)} reshape(bf16[48,49,16,32]{1,0,3,2:T(8,128)(2,1)} %copy.148) | data formatting | bytes 4816896 | tf_op jit(solution)/shard_map/mul | solution.py:229
  604.2 5.9 fusion.54
  610.2 11.0 %fusion.42 = f32[2048,512]{1,0:T(8,128)} fusion(bf16[2352,2048]{1,0:T(8,128)(2,1)} %get-tuple-element.123, f32[2352,512]{1,0:T(8,128)} %reshape.409, f32[2352]{0:T(1024)S(1)} %copy-done.32), kind=kOutput, calls=%fused_computation.125 | convolution fusion | flops 4934909952 | bytes 18654400 | tf_op jit(solution)/shard_map/dot_general | solution.py:197
  621.6 13.1 %fusion.25 = f32[512,2048]{1,0:T(8,128)} fusion(bf16[2352,2048]{1,0:T(8,128)(2,1)} %get-tuple-element.131, f32[2352,512]{1,0:T(8,128)} %add.283, f32[512]{0:T(512)S(1)} %bitcast.126, f32[512]{0:T(512)S(1)} %bitcast.118, f32[2352]{0:T(1024)S(1)} %copy-done.28, f32[2352]{0:T(1024)S(1)} %copy-done.30), kind=kOutput, calls=%fused_computation.57 | convolution fusion | flops 4938522624 | bytes 18667904 | tf_op jit(solution)/shard_map/dot_general | solution.py:202
  637.7 5.2 all-gather.9
  644.0 9.3 %convolution_convert_fusion = bf16[2352,512]{1,0:T(8,128)(2,1)} fusion(bf16[2352,1536]{0,1:T(8,128)(2,1)} %copy-done.23, bf16[512,1536]{1,0:T(8,128)(2,1)} %all-gather.14.cloned.1.call-done), kind=kOutput, calls=%fused_computation.74 | convolution fusion | flops 3700580352 | bytes 11206656 | tf_op jit(solution)/shard_map/dot_general | solution.py:244
  662.7 10.6 %multiply_convert_fusion.1 = bf16[2352,512]{1,0:T(8,128)(2,1)} fusion(f32[2352,512]{1,0:T(8,128)S(1)} %bitcast.102, bf16[2352,2048]{1,0:T(8,128)(2,1)} %get-tuple-element.123, bf16[2048,512]{1,0:T(8,128)(2,1)S(1)} %copy-done.55, f32[512]{0:T(512)S(1)} %bitcast.128, f32[2352]{0:T(1024)S(1)} %copy-done.32), kind=kOutput, calls=%fused_computation.61 | convolution fusion | flops 4937318400 | bytes 18967744 | tf_op jit(solution)/shard_map/dot_general | solution.py:192
  681.2 15.3 %reduce-scatter.11.cloned.1.call-done = f32[512,512]{1,0:T(8,128)} async-done(((f32[2048,512]{1,0:T(8,128)}), f32[512,512]{1,0:T(8,128)}) %reduce-scatter.11.cloned.1.call-update) | async-done | bytes 1048592 | tf_op jit(solution)/shard_map/reduce_scatter | solution.py:289
  696.5 47.1 %reduce-scatter.9.cloned.1.call-done = f32[128,2048]{1,0:T(8,128)} async-done(((f32[512,2048]{1,0:T(8,128)}), f32[128,2048]{1,0:T(8,128)}) %reduce-scatter.9.cloned.1.call-update) | async-done | bytes 1048592 | tf_op jit(solution)/shard_map/reduce_scatter | solution.py:287
  743.7 5.9 bitcast_reduce_fusion
  750.6 5.3 multiply_reduce_fusion.4
  755.9 11.6 %all-reduce.12 = (f32[512]{0:T(512)S(1)}, f32[512]{0:T(512)S(1)}, f32[512]{0:T(512)S(1)}, f32[512]{0:T(512)S(1)}, f32[16,169]{1,0:T(8,128)S(1)}, /*index=5*/f32[...) all-reduce(f32[512]{0:T(512)S(1)} %get-tuple-element.82, ...), channel_id=2, replica_groups=mesh['band'=2,'img'=4,'fsdp'=4] {'fsdp'}, use_global_device_ids=true, to_apply=%region_13.14.clone | all-reduce | flops 8848 | bytes 70784
  773.6 6.4 reshape.421
  780.1 8.1 multiply_add_fusion
  788.2 6.3 reshape.418
  794.4 7.8 copy.162
  802.3 37.5 %all-reduce.10 = (f32[128]{0:T(128)}, f32[128]{0:T(128)}, f32[128]{0:T(128)}, f32[128]{0:T(128)}, f32[4,169]{1,0:T(4,128)}, /*index=5*/f32[128]{0:T(128)}, f32[1...) all-reduce(f32[128]{0:T(128)S(1)} %dynamic-slice.1, ...), channel_id=1, replica_groups=mesh['band'=2,'img'=4,'fsdp'=4] {'band','img'}, use_global_device_ids=true, to_apply=%region_12.13 | all-reduce | flops 2212 | bytes 17696 | tf_op jit(solution)/shard_map/psum | solution.py:257
  839.8 36.6 %all-reduce.15.cloned.1.call-done = (f32[128,1536]{1,0:T(8,128)}, f32[128,512]{1,0:T(8,128)}, f32[128,2048]{1,0:T(8,128)}, f32[512,512]{1,0:T(8,128)}) async-done(((f32[128,1536]{1,0:T(8,128)}, f32[128,512]{1,0:T(8,128)}, f32[128,2048]{1,0:T(8,128)}, f32[512,512]{1,0:T(8,128)}), (f32[128,1536]{1,0:T(8,128)}, f32[128,512]{1,0:T(8,128)}, f32[128,2048]{1,0:T(8,128)}, ...) | async-done | bytes 3145744 | tf_op jit(solution)/shard_map/psum | solution.py:257
  (268 shorter events, 116.3 us)
Async XLA Ops:
  7.2 17.4 %copy-start = (bf16[24,7,14,512]{3,0,2,1:T(8,128)(2,1)S(1)}, bf16[24,7,14,512]{3,0,2,1:T(8,128)(2,1)}, u32[]{:S(2)}) copy-start(bf16[24,7,14,512]{3,0,2,1:T(8,128)(2,1)} %param.17) | copy-start | bytes 7225348
  7.2 65.9 %all-gather.14.cloned.1.call-start = ((), (), s32[]{:S(2)}) async-start(), calls=%async_computation.4 | async-start | bytes 1966080 | tf_op jit(solution)/shard_map/all_gather | solution.py:132
  7.9 292.1 %all-gather.16.cloned.1.call-start = ((), (), s32[]{:S(2)}) async-start(), calls=%async_computation.5 | async-start | bytes 2621440 | tf_op jit(solution)/shard_map/all_gather | solution.py:140
  14.2 11.5 %copy-start.33 = (f32[4,1,128]{2,1,0:T(1,128)}, f32[4,1,128]{2,1,0:T(1,128)S(1)}, u32[]{:S(2)}) copy-start(f32[4,1,128]{2,1,0:T(1,128)S(1)} %convert_element_type.153) | copy-start | bytes 6148
  21.8 6.4 copy-start.18
  24.6 8.1 copy-start.49
  24.6 13.1 %copy-start.50 = (bf16[128]{0:T(256)(128)(2,1)S(1)}, bf16[128]{0:T(256)(128)(2,1)}, u32[]{:S(2)}) copy-start(bf16[128]{0:T(256)(128)(2,1)} %param.24) | copy-start | bytes 772
  24.7 18.1 %copy-start.51 = (bf16[128]{0:T(256)(128)(2,1)S(1)}, bf16[128]{0:T(256)(128)(2,1)}, u32[]{:S(2)}) copy-start(bf16[128]{0:T(256)(128)(2,1)} %param.27) | copy-start | bytes 772
  24.7 23.3 %copy-start.43 = (bf16[4,169]{1,0:T(4,128)(2,1)S(1)}, bf16[4,169]{1,0:T(4,128)(2,1)}, u32[]{:S(2)}) copy-start(bf16[4,169]{1,0:T(4,128)(2,1)} %param.25) | copy-start | bytes 4060
  27.2 27.6 %copy-start.26 = (bf16[128,512]{1,0:T(8,128)(2,1)S(1)}, bf16[128,512]{1,0:T(8,128)(2,1)}, u32[]{:S(2)}) copy-start(bf16[128,512]{1,0:T(8,128)(2,1)} %param.26) | copy-start | bytes 393220
  28.2 34.5 %collective-permute-start = (bf16[24,3,14,512]{3,0,2,1:T(8,128)(2,1)}, bf16[24,3,14,512]{3,0,2,1:T(8,128)(2,1)}, u32[]{:S(2)}, u32[]{:S(2)}) collective-permute-start(bf16[24,3,14,512]{3,0,2,1:T(8,128)(2,1)} %slice.82), channel_id=1, source_target_pairs={{0,16},{16,0},{1,17},{17,1},{2,18},{18,2},{3,19},{19,3},{4,20},{20... | collective-permute-start | bytes 3096584 | tf_op jit(solution)/shard_map/ppermute | solution.py:19
  30.0 319.9 %all-gather.18.cloned.1.call-start = ((), (), s32[]{:S(2)}) async-start(), calls=%async_computation.6 | async-start | bytes 2621440 | tf_op jit(solution)/shard_map/all_gather | solution.py:142
  54.7 132.9 %copy-start.2 = (f32[16,49,49]{1,2,0:T(8,128)}, f32[16,49,49]{1,2,0:T(8,128)S(1)}, u32[]{:S(2)}) copy-start(f32[16,49,49]{1,2,0:T(8,128)S(1)} %copy.129) | copy-start | bytes 460996
  54.7 9.6 %copy-start.12 = (bf16[24,4,14,512]{3,0,2,1:T(8,128)(2,1)S(1)}, bf16[24,4,14,512]{3,0,2,1:T(8,128)(2,1)}, u32[]{:S(2)}) copy-start(bf16[24,4,14,512]{3,0,2,1:T(8,128)(2,1)} %slice.81) | copy-start | bytes 4128772
  134.9 52.7 %copy-start.6 = (pred[24,2,49,49]{2,3,1,0:T(8,128)(4,1)}, pred[24,2,49,49]{2,3,1,0:T(8,128)(4,1)S(1)}, u32[]{:S(2)}) copy-start(pred[24,2,49,49]{2,3,1,0:T(8,128)(4,1)S(1)} %broadcast_in_dim.38) | copy-start | bytes 345748
  211.5 9.2 %copy-start.24 = (bf16[512,512]{1,0:T(8,128)(2,1)S(1)}, bf16[512,512]{1,0:T(8,128)(2,1)}, u32[]{:S(2)}) copy-start(bf16[512,512]{1,0:T(8,128)(2,1)} %all_gather.48) | copy-start | bytes 1572868
  236.1 9.0 %copy-start.53 = (bf16[128]{0:T(256)(128)(2,1)S(1)}, bf16[128]{0:T(256)(128)(2,1)}, u32[]{:S(2)}) copy-start(bf16[128]{0:T(256)(128)(2,1)} %param.29) | copy-start | bytes 772
  236.1 14.0 %copy-start.48 = (bf16[512]{0:T(512)(128)(2,1)S(1)}, bf16[512]{0:T(512)(128)(2,1)}, u32[]{:S(2)}) copy-start(bf16[512]{0:T(512)(128)(2,1)} %param.31) | copy-start | bytes 3076
  236.1 19.5 %copy-start.57 = (s32[1,24]{1,0:T(1,128)S(1)}, s32[1,24]{1,0:T(1,128)}, u32[]{:S(2)}) copy-start(s32[1,24]{1,0:T(1,128)} %param.18) | copy-start | bytes 292
  236.1 37.8 %collective-permute-start.1 = (bf16[24,3,14,512]{3,0,2,1:T(8,128)(2,1)}, bf16[24,3,14,512]{3,0,2,1:T(8,128)(2,1)}, u32[]{:S(2)}, u32[]{:S(2)}) collective-permute-start(bf16[24,3,14,512]{3,0,2,1:T(8,128)(2,1)} %pad_maximum_fusion.5), channel_id=1, source_target_pairs={{0,16},{16,0},{1,17},{17,1},{2,18},{18,2},{3,19},{19,3},{4,20},{20... | collective-permute-start | bytes 3096584 | tf_op jit(solution)/shard_map/ppermute | solution.py:19
  236.6 444.6 %reduce-scatter.7.cloned.1.call-start = ((), (), s32[]{:S(2)}) async-start(), calls=%async_computation.8 | async-start | bytes 1310720 | tf_op jit(solution)/shard_map/reduce_scatter | solution.py:283
  245.1 135.2 %copy-start.38 = (f32[4,1,128]{2,1,0:T(1,128)}, f32[4,1,128]{2,1,0:T(1,128)S(1)}, u32[]{:S(2)}) copy-start(f32[4,1,128]{2,1,0:T(1,128)S(1)} %convert_element_type.158) | copy-start | bytes 6148
  250.1 49.9 %copy-start.46 = (f32[4,1,128]{2,1,0:T(1,128)}, f32[4,1,128]{2,1,0:T(1,128)S(1)}, u32[]{:S(2)}) copy-start(f32[4,1,128]{2,1,0:T(1,128)S(1)} %convert_element_type.159) | copy-start | bytes 6148
  255.6 12.0 %copy-start.41 = (f32[24]{0:T(128)}, f32[24]{0:T(128)S(1)}, u32[]{:S(2)}) copy-start(f32[24]{0:T(128)S(1)} %convert_bitcast_fusion.2) | copy-start | bytes 292
  279.2 101.2 %copy-start.27 = (f32[2352]{0:T(1024)}, f32[2352]{0:T(1024)S(1)}, u32[]{:S(2)}) copy-start(f32[2352]{0:T(1024)S(1)} %rsqrt.25) | copy-start | bytes 28228
  279.3 101.0 %copy-start.29 = (f32[2352]{0:T(1024)}, f32[2352]{0:T(1024)S(1)}, u32[]{:S(2)}) copy-start(f32[2352]{0:T(1024)S(1)} %div.52) | copy-start | bytes 28228
  300.0 49.9 %copy-start.31 = (f32[2352]{0:T(1024)S(1)}, f32[2352]{0:T(1024)}, u32[]{:S(2)}) copy-start(f32[2352]{0:T(1024)} %mul.209) | copy-start | bytes 28228
  349.9 18.1 %copy-start.9 = (f32[2352,512]{1,0:T(8,128)S(1)}, f32[2352,512]{1,0:T(8,128)}, u32[]{:S(2)}) copy-start(f32[2352,512]{1,0:T(8,128)} %add.283) | copy-start | bytes 14450692
  349.9 18.1 %copy-start.56 = (bf16[512,2048]{1,0:T(8,128)(2,1)S(1)}, bf16[512,2048]{1,0:T(8,128)(2,1)}, u32[]{:S(2)}) copy-start(bf16[512,2048]{1,0:T(8,128)(2,1)} %all-gather.16.cloned.1.call-done) | copy-start | bytes 6291460
  368.0 12.3 %copy-start.10 = (f32[2352,512]{1,0:T(8,128)S(1)}, f32[2352,512]{1,0:T(8,128)}, u32[]{:S(2)}) copy-start(f32[2352,512]{1,0:T(8,128)} %reshape.409) | copy-start | bytes 14450692
  391.6 25.1 %collective-permute-start.2 = (bf16[24,3,14,512]{3,0,2,1:T(8,128)(2,1)S(1)}, bf16[24,3,14,512]{3,0,2,1:T(8,128)(2,1)S(1)}, u32[]{:S(2)}, u32[]{:S(2)}) collective-permute-start(bf16[24,3,14,512]{3,0,2,1:T(8,128)(2,1)S(1)} %copy.139), channel_id=1, source_target_pairs={{0,16},{16,0},{1,17},{17,1},{2,18},{18,2},{3,19},{19,3},{4,20},{20... | collective-permute-start | bytes 3096584 | tf_op jit(solution)/shard_map/ppermute | solution.py:19
  423.5 5.1 copy-start.17
  423.5 5.1 copy-start.25
  442.9 13.6 %copy-start.3 = (f32[16,49,49]{1,2,0:T(8,128)S(1)}, f32[16,49,49]{1,2,0:T(8,128)}, u32[]{:S(2)}) copy-start(f32[16,49,49]{1,2,0:T(8,128)} %copy-done.2) | copy-start | bytes 460996
  442.9 13.6 %copy-start.7 = (pred[24,2,49,49]{2,3,1,0:T(8,128)(4,1)S(1)}, pred[24,2,49,49]{2,3,1,0:T(8,128)(4,1)}, u32[]{:S(2)}) copy-start(pred[24,2,49,49]{2,3,1,0:T(8,128)(4,1)} %copy-done.6) | copy-start | bytes 345748
  442.9 13.6 %copy-start.8 = (f32[48,16,49]{2,1,0:T(8,128)S(1)}, f32[48,16,49]{2,1,0:T(8,128)}, u32[]{:S(2)}) copy-start(f32[48,16,49]{2,1,0:T(8,128)} %log_add_fusion) | copy-start | bytes 451588
  456.6 63.9 %slice-start = ((s8[6291456]{0:T(1024)(128)(4,1)}), s8[2097152]{0:T(1024)(128)(4,1)S(1)}, s32[]{:S(2)}) async-start(s8[6291456]{0:T(1024)(128)(4,1)} %bitcast.93), calls=%async_computation.12 | async-start | bytes 4194304
  479.9 40.6 %slice-start.1 = ((s8[6291456]{0:T(1024)(128)(4,1)}), s8[4194304]{0:T(1024)(128)(4,1)S(1)}, s32[]{:S(2)}) async-start(s8[6291456]{0:T(1024)(128)(4,1)} %bitcast.93), calls=%async_computation.13 | async-start | bytes 8388608
  542.7 138.5 %reduce-scatter.5.cloned.1.call-start = ((), (), s32[]{:S(2)}) async-start(), calls=%async_computation.7 | async-start | bytes 3932160 | tf_op jit(solution)/shard_map/reduce_scatter | solution.py:279
  604.2 6.0 copy-start.32
  610.1 86.4 %reduce-scatter.11.cloned.1.call-start = ((), (), s32[]{:S(2)}) async-start(), calls=%async_computation.10 | async-start | bytes 5242880 | tf_op jit(solution)/shard_map/reduce_scatter | solution.py:289
  610.2 11.4 %copy-start.28 = (f32[2352]{0:T(1024)S(1)}, f32[2352]{0:T(1024)}, u32[]{:S(2)}) copy-start(f32[2352]{0:T(1024)} %copy-done.27) | copy-start | bytes 28228
  610.2 11.4 %copy-start.30 = (f32[2352]{0:T(1024)S(1)}, f32[2352]{0:T(1024)}, u32[]{:S(2)}) copy-start(f32[2352]{0:T(1024)} %copy-done.29) | copy-start | bytes 28228
  610.2 11.4 %copy-start.39 = (f32[4,1,128]{2,1,0:T(1,128)S(1)}, f32[4,1,128]{2,1,0:T(1,128)}, u32[]{:S(2)}) copy-start(f32[4,1,128]{2,1,0:T(1,128)} %copy-done.38) | copy-start | bytes 6148
  610.2 11.4 %copy-start.47 = (f32[4,1,128]{2,1,0:T(1,128)S(1)}, f32[4,1,128]{2,1,0:T(1,128)}, u32[]{:S(2)}) copy-start(f32[4,1,128]{2,1,0:T(1,128)} %copy-done.46) | copy-start | bytes 6148
  621.3 13.6 %copy-start.22 = (f32[24,7,14]{0,2,1:T(8,128)S(1)}, f32[24,7,14]{0,2,1:T(8,128)}, u32[]{:S(2)}) copy-start(f32[24,7,14]{0,2,1:T(8,128)} %copy-done.21) | copy-start | bytes 28228
  621.3 13.7 %copy-start.19 = (f32[24,7,14]{0,2,1:T(8,128)S(1)}, f32[24,7,14]{0,2,1:T(8,128)}, u32[]{:S(2)}) copy-start(f32[24,7,14]{0,2,1:T(8,128)} %copy-done.18) | copy-start | bytes 28228
  621.3 13.8 %copy-start.58 = (u32[32]{0:T(128)S(1)}, u32[32]{0:T(128)}, u32[]{:S(2)}) copy-start(u32[32]{0:T(128)} %constant.138) | copy-start | bytes 388
  621.3 16.4 %copy-start.54 = (bf16[128]{0:T(256)(128)(2,1)S(1)}, bf16[128]{0:T(256)(128)(2,1)}, u32[]{:S(2)}) copy-start(bf16[128]{0:T(256)(128)(2,1)} %param.33) | copy-start | bytes 772
  621.3 21.8 %copy-start.42 = (f32[24]{0:T(128)S(1)}, f32[24]{0:T(128)}, u32[]{:S(2)}) copy-start(f32[24]{0:T(128)} %copy-done.41) | copy-start | bytes 292
  621.3 122.3 %reduce-scatter.9.cloned.1.call-start = ((), (), s32[]{:S(2)}) async-start(), calls=%async_computation.9 | async-start | bytes 5242880 | tf_op jit(solution)/shard_map/reduce_scatter | solution.py:287
  634.7 8.4 copy-start.14
  634.8 241.7 %all-reduce.15.cloned.1.call-start = ((), (), s32[]{:S(2)}) async-start(), calls=%async_computation.11 | async-start | bytes 6291456 | tf_op jit(solution)/shard_map/psum | solution.py:257
  653.3 9.5 %slice-start.2 = ((s8[4816896]{0:T(1024)(128)(4,1)}), s8[622592]{0:T(1024)(128)(4,1)S(1)}, s32[]{:S(2)}) async-start(s8[4816896]{0:T(1024)(128)(4,1)} %bitcast.101), calls=%async_computation.14 | async-start | bytes 1245184
  657.1 5.7 slice-start.3
  661.1 89.4 %collective-permute-start.3 = (bf16[24,3,14,512]{3,0,2,1:T(8,128)(2,1)}, bf16[24,3,14,512]{3,0,2,1:T(8,128)(2,1)}, u32[]{:S(2)}, u32[]{:S(2)}) collective-permute-start(bf16[24,3,14,512]{3,0,2,1:T(8,128)(2,1)} %pad_maximum_fusion.4), channel_id=1, source_target_pairs={{0,16},{16,0},{1,17},{17,1},{2,18},{18,2},{3,19},{19,3},{4,20},{20... | collective-permute-start | bytes 3096584 | tf_op jit(solution)/shard_map/ppermute | solution.py:19
  743.7 6.0 copy-start.36
  743.7 6.9 copy-start.1
  743.7 6.9 copy-start.34
  749.5 6.4 copy-start.37
  749.5 6.4 copy-start.40
  749.5 6.4 copy-start.44
  749.5 6.4 copy-start.45
  876.4 6.1 copy-start.20
  (11 other events, 27.8 us)
Sparse Core Ops, SparseCore 0:
  9.6 22.3 all-gather.13
  33.5 22.6 all-gather.15
  236.7 23.8 all-gather.17
  542.8 26.1 reduce-scatter.6
  610.2 39.2 reduce-scatter.4
  651.9 44.5 reduce-scatter.10
  699.0 44.5 reduce-scatter.8
  747.5 128.8 all-reduce.14
where the time goes:
time: 901 us; the launch traced here: 891 us
  local copies, waits for them, and re-layouts  300 us (33%)
  matrix products  243 us (27%)
  waiting for transfers between devices  123 us (14%)
  blocking collectives  110 us (12%)
  other arithmetic  90.6 us (10%)
  between operations  17.6 us (2%)
    dot_general x1, matrix products, shards(): pre = jnp.dot(normed_two, weight_up, preferred_element_type=f32) + up_bias  49.9 us
    reduce_scatter x1, waiting for transfers between devices, shards(): lax.psum_scatter(s11, 'fsdp', scatter_dimension=0, tiled=True)  47.1 us
    psum x1, blocking collectives, shards(): lax.psum((grad_gain_one, grad_beta_one, grad_wqkv, grad_qbias, grad_vbias...  37.5 us
    psum x1, waiting for transfers between devices, shards(): lax.psum((grad_gain_one, grad_beta_one, grad_wqkv, grad_qbias, grad_vbias...  36.6 us
    unnamed x147, local copies, waits for them, and re-layouts  30.9 us
    reshape x2, local copies, waits for them, and re-layouts, shards(): grad_attended = jnp.dot(grad_proj, weight_out.T, preferred_element_type=f...  25.1 us
    reshape x2, local copies, waits for them, and re-layouts, shards(): ((qkv[:, :D] + query_bias) * scale).astype(bf16)  25 us
    reshape x2, local copies, waits for them, and re-layouts, shards(): (qkv[:, 2 * D:] + value_bias).astype(bf16)  25 us
  transfers between devices with their start and end apart: 12, of which 4 were waited for; matrix products, arithmetic and copies ran while one was open for 51% of the time, Pallas kernels for 0%

commit v1 on v0

--- a/solution.py
+++ b/solution.py
@@ -2,6 +2,7 @@
 import jax.numpy as jnp
 from jax import lax
 from jax.sharding import PartitionSpec as P
+from jax.lax import psum
 
 D = 512
 HEADS = 16
@@ -254,7 +255,13 @@
     grad_input = grad_resid + norm_back(grad_normed * gain_one, hat_one, rstd_one)
     final_output = output.reshape(slots, WIN, SIDE, D)
     final_grad = grad_input.reshape(slots, WIN, SIDE, D)
-    s01, s02, s03, s04, s05, s06, s07, s08, s09, s10, s11, s12, s13, s14 = lax.psum(
+
+    def proceed_clusters_all(arr):
+        for dev_j in ("img", "band"):
+            arr = psum(arr, axis_name=dev_j)
+        return arr
+
+    s01, s02, s03, s04, s05, s06, s07, s08, s09, s10, s11, s12, s13, s14 = proceed_clusters_all(
         (
             grad_gain_one,
             grad_beta_one,
@@ -270,8 +277,7 @@
             grad_upb,
             grad_down,
             grad_downb,
-        ),
-        ("band", "img"),
+        )
     )
     r01, r02, r03, r04, r05, r06, r07, r08, r09, r10, r11, r12, r13, r14 = (
         lax.psum_scatter(s01, "fsdp", scatter_dimension=0, tiled=True),

time: 901 us -> 979 us (1.087)
  waiting for transfers between devices: 123 us -> 212 us
  blocking collectives: 110 us -> 99.1 us
    psum x1 -> x2, waiting for transfers between devices: 36.6 us -> 88.6 us  [proceed_clusters_all(): arr = psum(arr, axis_name=dev_j)]
    reduce_scatter x1, waiting for transfers between devices: 15.3 us -> 47 us  [shards(): lax.psum_scatter(s13, 'fsdp', scatter_dimension=0, tiled=True)]
    psum x1 -> x2, blocking collectives: 37.5 us -> 26 us  [proceed_clusters_all(): arr = psum(arr, axis_name=dev_j)]
  transfers between devices with their start and end apart: 12 -> 13, of which waited for: 4 -> 6; matrix products, arithmetic and copies ran while one was open for 51% -> 47% of each run, Pallas kernels for 0% -> 0%
where the time goes in v1:
time: 979 us; the launch traced here: 969 us
  local copies, waits for them, and re-layouts  301 us (31%)
  matrix products  243 us (25%)
  waiting for transfers between devices  212 us (22%)
  blocking collectives  99.1 us (10%)
  other arithmetic  90.7 us (9%)
  between operations  17.3 us (2%)
    psum x2, waiting for transfers between devices, proceed_clusters_all(): arr = psum(arr, axis_name=dev_j)  88.6 us
    dot_general x1, matrix products, shards(): pre = jnp.dot(normed_two, weight_up, preferred_element_type=f32) + up_bias  49.9 us
    reduce_scatter x1, waiting for transfers between devices, shards(): lax.psum_scatter(s11, 'fsdp', scatter_dimension=0, tiled=True)  47.1 us
    reduce_scatter x1, waiting for transfers between devices, shards(): lax.psum_scatter(s13, 'fsdp', scatter_dimension=0, tiled=True)  47 us
    unnamed x147, local copies, waits for them, and re-layouts  31.3 us
    psum x2, blocking collectives, proceed_clusters_all(): arr = psum(arr, axis_name=dev_j)  26 us
    reshape x2, local copies, waits for them, and re-layouts, shards(): grad_attended = jnp.dot(grad_proj, weight_out.T, preferred_element_type=f...  25.1 us
    reshape x2, local copies, waits for them, and re-layouts, shards(): ((qkv[:, :D] + query_bias) * scale).astype(bf16)  25 us
  transfers between devices with their start and end apart: 13, of which 6 were waited for; matrix products, arithmetic and copies ran while one was open for 47% of the time, Pallas kernels for 0%

profile of v1, /device:TPU:0, one launch (start us, length us, event | category | flops | bytes accessed | tf_op | source)
XLA Modules:
  0.0 969.3 jit_solution(13817478064361988633)
XLA Ops:
  8.0 6.2 all-gather
  14.2 5.4 all-gather.1
  32.7 5.0 all-gather.3
  42.8 5.2 all-gather.5
  48.0 5.4 all-gather.4
  54.8 7.9 all_gather.48
  68.0 5.2 reshape.401
  73.1 6.2 fusion.53
  84.7 11.5 %reshape.462 = bf16[48,49,16,32]{3,2,1,0:T(8,128)(2,1)} reshape(bf16[2352,512]{1,0:T(8,128)(2,1)} %get-tuple-element.131) | data formatting | bytes 4816896 | tf_op jit(solution)/shard_map/reshape | solution.py:172
  96.2 13.5 %copy.127 = bf16[48,49,16,32]{1,3,2,0:T(8,128)(2,1)} copy(bf16[48,49,16,32]{3,2,1,0:T(8,128)(2,1)} %reshape.462) | data formatting | bytes 4816896 | tf_op jit(solution)/shard_map/reshape | solution.py:172
  109.8 11.5 %reshape.463 = bf16[48,49,16,32]{3,2,1,0:T(8,128)(2,1)} reshape(bf16[2352,512]{1,0:T(8,128)(2,1)} %slice.113) | data formatting | bytes 4816896 | tf_op jit(solution)/shard_map/reshape | solution.py:173
  121.3 13.5 %copy.128 = bf16[48,49,16,32]{1,3,2,0:T(8,128)(2,1)} copy(bf16[48,49,16,32]{3,2,1,0:T(8,128)(2,1)} %reshape.463) | data formatting | bytes 4816896 | tf_op jit(solution)/shard_map/reshape | solution.py:173
  134.9 13.4 %fusion.15 = (f32[48,16,49]{2,1,0:T(8,128)S(1)}, f32[48,16,49,49]{2,3,1,0:T(8,128)}) fusion(f32[16,49,49]{1,2,0:T(8,128)S(1)} %copy.129, pred[48,49,49]{1,2,0:T(8,128)(4,1)S(1)} %bitcast.95, bf16[48,49,16,32]{1,3,2,0:T(8,128)(2,1)} %copy.127, bf16[48,49,16,32]{1,3,2,0:T(8,128)(2,1)} %copy.128), kind=kOutput, calls=%fused_computation.30 | convolution fusion | flops 123508224 | bytes 12612208 | tf_op jit(solution)/shard_map/wqhd,wkhd->whqk/dot_general | solution.py:87
  148.3 13.4 %exponential_reduce_fusion = f32[48,16,49]{2,1,0:T(8,128)S(1)} fusion(f32[48,16,49,49]{2,3,1,0:T(8,128)} %get-tuple-element.136, f32[48,16,49]{2,1,0:T(8,128)S(1)} %get-tuple-element.135, f32[16,49,49]{1,2,0:T(8,128)S(1)} %copy.129, pred[48,49,49]{1,2,0:T(8,128)(4,1)S(1)} %bitcast.96), kind=kLoop, calls=%fused_computation.5 | loop fusion | flops 7338240 | bytes 7945840 | tf_op jit(solution)/shard_map/reduce_sum | solution.py:177
  162.5 11.5 %reshape.461 = bf16[48,49,16,32]{3,2,1,0:T(8,128)(2,1)} reshape(bf16[2352,512]{1,0:T(8,128)(2,1)} %get-tuple-element.132) | data formatting | bytes 4816896 | tf_op jit(solution)/shard_map/reshape | solution.py:174
  174.0 13.5 %copy.130 = bf16[48,49,16,32]{1,3,2,0:T(8,128)(2,1)} copy(bf16[48,49,16,32]{3,2,1,0:T(8,128)(2,1)} %reshape.461) | data formatting | bytes 4816896 | tf_op jit(solution)/shard_map/reshape | solution.py:174
  187.6 14.4 %convert_bitcast_fusion.1 = bf16[48,49,16,32]{1,3,2,0:T(8,128)(2,1)} fusion(bf16[48,49,16,32]{1,3,2,0:T(8,128)(2,1)} %copy.130, f32[48,16,49,49]{2,3,1,0:T(8,128)} %get-tuple-element.136, f32[48,16,49]{2,1,0:T(8,128)} %log_add_fusion, f32[16,49,49]{1,2,0:T(8,128)S(1)} %copy.129, pred[48,49,49]{1,2,0:T(8,128)(4,1)S(1)} %bitcast.97), kind=kOutput, calls=%fused_computation.38 | convolution fusion | flops 126594048 | bytes 12612208 | tf_op jit(solution)/shard_map/whqk,wkhd->wqhd/dot_general | solution.py:180
  201.9 9.5 copy.132
  211.5 9.2 reshape.405
  225.2 5.1 reshape.406
  245.1 5.1 all-gather.7
  250.1 5.4 all-gather.8
  261.2 6.3 reshape.409
  267.6 6.3 reshape.399
  281.2 5.3 copy.134
  286.5 6.4 reshape.420
  292.9 7.1 add.311
  300.0 49.9 %fusion.2 = (bf16[2352,2048]{1,0:T(8,128)(2,1)}, f32[2352,2048]{1,0:T(8,128)}) fusion(f32[2048]{0:T(1024)S(1)} %bitcast.122, bf16[512,2048]{1,0:T(8,128)(2,1)} %all-gather.16.cloned.1.call-done, f32[2352,512]{1,0:T(8,128)} %add.311, f32[512]{0:T(512)S(1)} %bitcast.125, f32[512]{0:T(512)S(1)} %bitcast.115, f32[2352]{0:T(1024)S(1)} %rsqrt.25, f32[2352]{0:T(1024)S(1)} %div.52), kind=kOutput, calls=%fused_computation.9 | convolution fusion | flops 5256437760 | bytes 35846528 | tf_op jit(solution)/shard_map/dot_general | solution.py:191
  349.9 18.1 %fusion.50 = (f32[2048]{0:T(1024)}, bf16[2352,2048]{1,0:T(8,128)(2,1)}) fusion(f32[2352,2048]{1,0:T(8,128)} %get-tuple-element.138, f32[2048]{0:T(1024)S(1)} %bitcast.123, bf16[2048,512]{1,0:T(8,128)(2,1)} %all-gather.18.cloned.1.call-done, f32[2352,512]{1,0:T(8,128)} %reshape.409, f32[2352]{0:T(1024)S(1)} %copy-done.31), kind=kOutput, calls=%fused_computation.130 | convolution fusion | flops 4992710656 | bytes 35841216 | tf_op jit(solution)/shard_map/dot_general | solution.py:200
  368.0 12.3 %multiply_reduce_fusion.3 = (f32[512]{0:T(512)}, f32[2352]{0:T(1024)S(1)}, f32[2352]{0:T(1024)S(1)}, f32[512]{0:T(512)}, f32[2352,512]{1,0:T(8,128)S(1)}) fusion(f32[2352,512]{1,0:T(8,128)S(1)} %copy-done.9, f32[2352]{0:T(1024)S(1)} %rsqrt.25, f32[2352]{0:T(1024)S(1)} %div.52, f32[512]{0:T(512)S(1)} %bitcast.116, bf16[512,2048]{1,0:T(8,128)(2,1)S(1)} %copy-done.56, ...), kind=kOutput, calls=%fused_computation.51 | convolution fusion | flops 4943333376 | bytes 21408512 | tf_op jit(solution)/shard_map/dot_general | solution.py:204
  393.5 23.3 %collective-permute-done.2 = bf16[24,3,14,512]{3,0,2,1:T(8,128)(2,1)S(1)} collective-permute-done((bf16[24,3,14,512]{3,0,2,1:T(8,128)(2,1)S(1)}, bf16[24,3,14,512]{3,0,2,1:T(8,128)(2,1)S(1)}, u32[]{:S(2)}, u32[]{:S(2)}) %collective-permute-start.2) | collective-permute-done | bytes 1032224 | tf_op jit(solution)/shard_map/ppermute | solution.py:20
  423.5 5.1 fusion.55
  431.4 11.5 %reshape.464 = bf16[48,49,16,32]{3,2,1,0:T(8,128)(2,1)} reshape(bf16[2352,512]{1,0:T(8,128)(2,1)} %convolution_convert_fusion.1) | data formatting | bytes 4816896 | tf_op jit(solution)/shard_map/reshape | solution.py:218
  442.9 13.6 %copy.144 = bf16[48,49,16,32]{1,3,2,0:T(8,128)(2,1)} copy(bf16[48,49,16,32]{3,2,1,0:T(8,128)(2,1)} %reshape.464) | data formatting | bytes 4816896 | tf_op jit(solution)/shard_map/reshape | solution.py:218
  456.6 23.3 %multiply_reduce_fusion = (f32[48,16,49]{2,1,0:T(8,128)S(1)}, f32[48,16,49,49]{2,3,1,0:T(8,128)}) fusion(f32[48,16,49,49]{2,3,1,0:T(8,128)} %get-tuple-element.136, f32[48,16,49]{2,1,0:T(8,128)S(1)} %copy-done.8, f32[16,49,49]{1,2,0:T(8,128)S(1)} %copy-done.3, pred[48,49,49]{1,2,0:T(8,128)(4,1)S(1)} %bitcast.98, bf16[48,49,16,32]{1,3,2,0:T(8,128)(2,1)} %copy.144, ...), kind=kOutput, calls=%fused_computation.3 | convolution fusion | flops 127196160 | bytes 20138608 | tf_op jit(solution)/shard_map/wqhd,wkhd->whqk/dot_general | solution.py:221
  479.9 19.4 %bitcast_convert_fusion = (bf16[48,49,16,32]{1,3,2,0:T(8,128)(2,1)}, f32[48,16,32,49]{3,2,1,0:T(8,128)}) fusion(bf16[48,49,16,32]{1,3,2,0:T(8,128)(2,1)} %copy.144, f32[48,16,49,49]{2,3,1,0:T(8,128)} %get-tuple-element.136, f32[48,16,49]{2,1,0:T(8,128)S(1)} %copy-done.8, f32[16,49,49]{1,2,0:T(8,128)S(1)} %copy-done.3, pred[48,49,49]{1,2,0:T(8,128)(4,1)S(1)} %bitcast.99), kind=kOutput, calls=%fused_computation.32 | convolution fusion | flops 126594048 | bytes 17429104 | tf_op jit(solution)/shard_map/whqk,wqhd->wkhd/dot_general | solution.py:238
  499.2 21.2 %fusion.48 = (f32[16,49,49]{1,2,0:T(8,128)}, bf16[48,16,49,49]{2,3,1,0:T(8,128)(2,1)}) fusion(f32[48,16,49,49]{2,3,1,0:T(8,128)} %get-tuple-element.141, f32[48,16,49]{2,1,0:T(8,128)S(1)} %get-tuple-element.140, f32[48,16,49]{2,1,0:T(8,128)S(1)} %copy-done.8, f32[48,16,49,49]{2,3,1,0:T(8,128)} %get-tuple-element.136, f32[16,49,49]{1,2,0:T(8,128)S(1)} %copy-done.3, ...), kind=kLoop, calls=%fused_computation.129 | loop fusion | flops 12869360 | bytes 19163312 | tf_op jit(solution)/shard_map/reduce_sum | solution.py:224
  520.4 10.4 %convert_bitcast_fusion = bf16[48,49,16,32]{1,3,2,0:T(8,128)(2,1)} fusion(bf16[48,49,16,32]{1,3,2,0:T(8,128)(2,1)S(1)} %bitcast.94, bf16[48,16,49,49]{2,3,1,0:T(8,128)(2,1)} %get-tuple-element.129), kind=kOutput, calls=%fused_computation.37 | convolution fusion | flops 119218176 | bytes 8504832 | tf_op jit(solution)/shard_map/whqk,wqhd->wkhd/dot_general | solution.py:235
  530.8 11.9 %multiply_reduce_fusion.1 = (f32[16,32]{1,0:T(8,128)S(1)}, bf16[48,49,16,32]{1,3,2,0:T(8,128)(2,1)}) fusion(bf16[48,49,16,32]{1,3,2,0:T(8,128)(2,1)} %copy.128, bf16[48,16,49,49]{2,3,1,0:T(8,128)(2,1)} %get-tuple-element.129), kind=kOutput, calls=%fused_computation.33 | convolution fusion | flops 121626112 | bytes 8506880 | tf_op jit(solution)/shard_map/whqk,wkhd->wqhd/dot_general | solution.py:230
  542.8 9.6 copy.151
  552.3 8.5 reshape.414
  560.8 9.6 copy.154
  570.4 9.2 reshape.415
  579.6 9.4 copy.148
  589.0 9.3 mul.250
  604.2 5.9 fusion.54
  610.2 11.0 %fusion.42 = f32[2048,512]{1,0:T(8,128)} fusion(bf16[2352,2048]{1,0:T(8,128)(2,1)} %get-tuple-element.137, f32[2352,512]{1,0:T(8,128)} %reshape.409, f32[2352]{0:T(1024)S(1)} %copy-done.32), kind=kOutput, calls=%fused_computation.125 | convolution fusion | flops 4934909952 | bytes 18654400 | tf_op jit(solution)/shard_map/dot_general | solution.py:198
  621.6 13.1 %fusion.25 = f32[512,2048]{1,0:T(8,128)} fusion(bf16[2352,2048]{1,0:T(8,128)(2,1)} %get-tuple-element.145, f32[2352,512]{1,0:T(8,128)} %add.311, f32[512]{0:T(512)S(1)} %bitcast.126, f32[512]{0:T(512)S(1)} %bitcast.118, f32[2352]{0:T(1024)S(1)} %copy-done.28, f32[2352]{0:T(1024)S(1)} %copy-done.30), kind=kOutput, calls=%fused_computation.57 | convolution fusion | flops 4938522624 | bytes 18667904 | tf_op jit(solution)/shard_map/dot_general | solution.py:203
  637.7 5.2 all-gather.9
  644.0 5.5 reduce-scatter.5.cloned.1.call-done
  649.5 47.0 %reduce-scatter.11.cloned.1.call-done = f32[512,512]{1,0:T(8,128)} async-done(((f32[2048,512]{1,0:T(8,128)}), f32[512,512]{1,0:T(8,128)}) %reduce-scatter.11.cloned.1.call-update) | async-done | bytes 1048592 | tf_op jit(solution)/shard_map/reduce_scatter | solution.py:295
  696.5 47.1 %reduce-scatter.9.cloned.1.call-done = f32[128,2048]{1,0:T(8,128)} async-done(((f32[512,2048]{1,0:T(8,128)}), f32[128,2048]{1,0:T(8,128)}) %reduce-scatter.9.cloned.1.call-update) | async-done | bytes 1048592 | tf_op jit(solution)/shard_map/reduce_scatter | solution.py:293
  743.7 9.2 convolution_convert_fusion
  762.2 10.6 %multiply_convert_fusion.1 = bf16[2352,512]{1,0:T(8,128)(2,1)} fusion(f32[2352,512]{1,0:T(8,128)S(1)} %bitcast.102, bf16[2352,2048]{1,0:T(8,128)(2,1)} %get-tuple-element.137, bf16[2048,512]{1,0:T(8,128)(2,1)S(1)} %copy-done.55, f32[512]{0:T(512)S(1)} %bitcast.128, f32[2352]{0:T(1024)S(1)} %copy-done.32), kind=kOutput, calls=%fused_computation.61 | convolution fusion | flops 4937318400 | bytes 18967744 | tf_op jit(solution)/shard_map/dot_general | solution.py:193
  780.7 86.7 %all-reduce.18.cloned.1.call-done = (f32[128,1536]{1,0:T(8,128)}, f32[128,512]{1,0:T(8,128)}, f32[128,2048]{1,0:T(8,128)}, f32[512,512]{1,0:T(8,128)}) async-done(((f32[128,1536]{1,0:T(8,128)}, f32[128,512]{1,0:T(8,128)}, f32[128,2048]{1,0:T(8,128)}, f32[512,512]{1,0:T(8,128)}), (f32[128,1536]{1,0:T(8,128)}, f32[128,512]{1,0:T(8,128)}, f32[128,2048]{1,0:T(8,128)}, ...) | async-done | bytes 3145744 | tf_op jit(solution)/shard_map/psum | solution.py:261
  867.4 5.9 bitcast_reduce_fusion
  874.3 5.5 multiply_reduce_fusion.4
  879.9 12.3 %all-reduce.10 = (f32[512]{0:T(512)S(1)}, f32[512]{0:T(512)S(1)}, f32[512]{0:T(512)S(1)}, f32[512]{0:T(512)S(1)}, f32[16,169]{1,0:T(8,128)S(1)}, /*index=5*/f32[...) all-reduce(f32[512]{0:T(512)S(1)} %get-tuple-element.82, ...), channel_id=2, replica_groups=mesh['band'=2,'img'=4,'fsdp'=4] {'fsdp'}, use_global_device_ids=true, to_apply=%region_14.15.clone | all-reduce | flops 8848 | bytes 70784
  898.3 6.4 reshape.421
  904.7 8.0 multiply_add_fusion
  912.6 6.3 reshape.418
  918.9 8.3 copy.162
  927.3 16.9 %all-reduce.11 = (f32[128]{0:T(128)S(1)}, f32[128]{0:T(128)S(1)}, f32[128]{0:T(128)S(1)}, f32[128]{0:T(128)S(1)}, f32[4,169]{1,0:T(4,128)S(1)}, /*index=5*/f32[1...) all-reduce(f32[128]{0:T(128)S(1)} %dynamic-slice.1, ...), channel_id=1, replica_groups=mesh['band'=2,'img'=4,'fsdp'=4] {'img'}, use_global_device_ids=true, to_apply=%region_12.13 | all-reduce | flops 2212 | bytes 17696 | tf_op jit(solution)/shard_map/psum | solution.py:261
  944.1 9.1 all-reduce.13
  (272 shorter events, 128.2 us)
Async XLA Ops:
  7.2 17.4 %copy-start = (bf16[24,7,14,512]{3,0,2,1:T(8,128)(2,1)S(1)}, bf16[24,7,14,512]{3,0,2,1:T(8,128)(2,1)}, u32[]{:S(2)}) copy-start(bf16[24,7,14,512]{3,0,2,1:T(8,128)(2,1)} %param.17) | copy-start | bytes 7225348
  7.2 65.9 %all-gather.14.cloned.1.call-start = ((), (), s32[]{:S(2)}) async-start(), calls=%async_computation.4 | async-start | bytes 1966080 | tf_op jit(solution)/shard_map/all_gather | solution.py:133
  7.9 292.1 %all-gather.16.cloned.1.call-start = ((), (), s32[]{:S(2)}) async-start(), calls=%async_computation.5 | async-start | bytes 2621440 | tf_op jit(solution)/shard_map/all_gather | solution.py:141
  14.2 11.5 %copy-start.33 = (f32[4,1,128]{2,1,0:T(1,128)}, f32[4,1,128]{2,1,0:T(1,128)S(1)}, u32[]{:S(2)}) copy-start(f32[4,1,128]{2,1,0:T(1,128)S(1)} %convert_element_type.153) | copy-start | bytes 6148
  21.8 6.4 copy-start.18
  24.6 8.1 copy-start.49
  24.6 13.1 %copy-start.50 = (bf16[128]{0:T(256)(128)(2,1)S(1)}, bf16[128]{0:T(256)(128)(2,1)}, u32[]{:S(2)}) copy-start(bf16[128]{0:T(256)(128)(2,1)} %param.24) | copy-start | bytes 772
  24.7 18.1 %copy-start.51 = (bf16[128]{0:T(256)(128)(2,1)S(1)}, bf16[128]{0:T(256)(128)(2,1)}, u32[]{:S(2)}) copy-start(bf16[128]{0:T(256)(128)(2,1)} %param.27) | copy-start | bytes 772
  24.7 23.3 %copy-start.43 = (bf16[4,169]{1,0:T(4,128)(2,1)S(1)}, bf16[4,169]{1,0:T(4,128)(2,1)}, u32[]{:S(2)}) copy-start(bf16[4,169]{1,0:T(4,128)(2,1)} %param.25) | copy-start | bytes 4060
  27.2 27.6 %copy-start.26 = (bf16[128,512]{1,0:T(8,128)(2,1)S(1)}, bf16[128,512]{1,0:T(8,128)(2,1)}, u32[]{:S(2)}) copy-start(bf16[128,512]{1,0:T(8,128)(2,1)} %param.26) | copy-start | bytes 393220
  28.2 34.5 %collective-permute-start = (bf16[24,3,14,512]{3,0,2,1:T(8,128)(2,1)}, bf16[24,3,14,512]{3,0,2,1:T(8,128)(2,1)}, u32[]{:S(2)}, u32[]{:S(2)}) collective-permute-start(bf16[24,3,14,512]{3,0,2,1:T(8,128)(2,1)} %slice.82), channel_id=1, source_target_pairs={{0,16},{16,0},{1,17},{17,1},{2,18},{18,2},{3,19},{19,3},{4,20},{20... | collective-permute-start | bytes 3096584 | tf_op jit(solution)/shard_map/ppermute | solution.py:20
  30.0 319.9 %all-gather.18.cloned.1.call-start = ((), (), s32[]{:S(2)}) async-start(), calls=%async_computation.6 | async-start | bytes 2621440 | tf_op jit(solution)/shard_map/all_gather | solution.py:143
  54.7 132.9 %copy-start.2 = (f32[16,49,49]{1,2,0:T(8,128)}, f32[16,49,49]{1,2,0:T(8,128)S(1)}, u32[]{:S(2)}) copy-start(f32[16,49,49]{1,2,0:T(8,128)S(1)} %copy.129) | copy-start | bytes 460996
  54.7 9.6 copy-start.12
  134.9 52.7 %copy-start.6 = (pred[24,2,49,49]{2,3,1,0:T(8,128)(4,1)}, pred[24,2,49,49]{2,3,1,0:T(8,128)(4,1)S(1)}, u32[]{:S(2)}) copy-start(pred[24,2,49,49]{2,3,1,0:T(8,128)(4,1)S(1)} %broadcast_in_dim.38) | copy-start | bytes 345748
  211.5 9.2 copy-start.24
  236.1 9.0 copy-start.53
  236.1 14.0 %copy-start.48 = (bf16[512]{0:T(512)(128)(2,1)S(1)}, bf16[512]{0:T(512)(128)(2,1)}, u32[]{:S(2)}) copy-start(bf16[512]{0:T(512)(128)(2,1)} %param.31) | copy-start | bytes 3076
  236.1 19.5 %copy-start.57 = (s32[1,24]{1,0:T(1,128)S(1)}, s32[1,24]{1,0:T(1,128)}, u32[]{:S(2)}) copy-start(s32[1,24]{1,0:T(1,128)} %param.18) | copy-start | bytes 292
  236.1 37.8 %collective-permute-start.1 = (bf16[24,3,14,512]{3,0,2,1:T(8,128)(2,1)}, bf16[24,3,14,512]{3,0,2,1:T(8,128)(2,1)}, u32[]{:S(2)}, u32[]{:S(2)}) collective-permute-start(bf16[24,3,14,512]{3,0,2,1:T(8,128)(2,1)} %pad_maximum_fusion.5), channel_id=1, source_target_pairs={{0,16},{16,0},{1,17},{17,1},{2,18},{18,2},{3,19},{19,3},{4,20},{20... | collective-permute-start | bytes 3096584 | tf_op jit(solution)/shard_map/ppermute | solution.py:20
  236.6 407.4 %reduce-scatter.7.cloned.1.call-start = ((), (), s32[]{:S(2)}) async-start(), calls=%async_computation.8 | async-start | bytes 1310720 | tf_op jit(solution)/shard_map/reduce_scatter | solution.py:289
  245.1 135.2 %copy-start.38 = (f32[4,1,128]{2,1,0:T(1,128)}, f32[4,1,128]{2,1,0:T(1,128)S(1)}, u32[]{:S(2)}) copy-start(f32[4,1,128]{2,1,0:T(1,128)S(1)} %convert_element_type.158) | copy-start | bytes 6148
  250.1 49.9 %copy-start.46 = (f32[4,1,128]{2,1,0:T(1,128)}, f32[4,1,128]{2,1,0:T(1,128)S(1)}, u32[]{:S(2)}) copy-start(f32[4,1,128]{2,1,0:T(1,128)S(1)} %convert_element_type.159) | copy-start | bytes 6148
  255.6 12.0 %copy-start.41 = (f32[24]{0:T(128)}, f32[24]{0:T(128)S(1)}, u32[]{:S(2)}) copy-start(f32[24]{0:T(128)S(1)} %convert_bitcast_fusion.2) | copy-start | bytes 292
  279.2 101.2 %copy-start.27 = (f32[2352]{0:T(1024)}, f32[2352]{0:T(1024)S(1)}, u32[]{:S(2)}) copy-start(f32[2352]{0:T(1024)S(1)} %rsqrt.25) | copy-start | bytes 28228
  279.3 101.0 %copy-start.29 = (f32[2352]{0:T(1024)}, f32[2352]{0:T(1024)S(1)}, u32[]{:S(2)}) copy-start(f32[2352]{0:T(1024)S(1)} %div.52) | copy-start | bytes 28228
  300.0 49.9 %copy-start.31 = (f32[2352]{0:T(1024)S(1)}, f32[2352]{0:T(1024)}, u32[]{:S(2)}) copy-start(f32[2352]{0:T(1024)} %mul.209) | copy-start | bytes 28228
  349.9 18.1 %copy-start.9 = (f32[2352,512]{1,0:T(8,128)S(1)}, f32[2352,512]{1,0:T(8,128)}, u32[]{:S(2)}) copy-start(f32[2352,512]{1,0:T(8,128)} %add.311) | copy-start | bytes 14450692
  349.9 18.1 %copy-start.56 = (bf16[512,2048]{1,0:T(8,128)(2,1)S(1)}, bf16[512,2048]{1,0:T(8,128)(2,1)}, u32[]{:S(2)}) copy-start(bf16[512,2048]{1,0:T(8,128)(2,1)} %all-gather.16.cloned.1.call-done) | copy-start | bytes 6291460
  368.0 12.3 %copy-start.10 = (f32[2352,512]{1,0:T(8,128)S(1)}, f32[2352,512]{1,0:T(8,128)}, u32[]{:S(2)}) copy-start(f32[2352,512]{1,0:T(8,128)} %reshape.409) | copy-start | bytes 14450692
  391.6 25.1 %collective-permute-start.2 = (bf16[24,3,14,512]{3,0,2,1:T(8,128)(2,1)S(1)}, bf16[24,3,14,512]{3,0,2,1:T(8,128)(2,1)S(1)}, u32[]{:S(2)}, u32[]{:S(2)}) collective-permute-start(bf16[24,3,14,512]{3,0,2,1:T(8,128)(2,1)S(1)} %copy.139), channel_id=1, source_target_pairs={{0,16},{16,0},{1,17},{17,1},{2,18},{18,2},{3,19},{19,3},{4,20},{20... | collective-permute-start | bytes 3096584 | tf_op jit(solution)/shard_map/ppermute | solution.py:20
  423.5 5.1 copy-start.17
  442.9 13.6 %copy-start.3 = (f32[16,49,49]{1,2,0:T(8,128)S(1)}, f32[16,49,49]{1,2,0:T(8,128)}, u32[]{:S(2)}) copy-start(f32[16,49,49]{1,2,0:T(8,128)} %copy-done.2) | copy-start | bytes 460996
  442.9 13.6 %copy-start.7 = (pred[24,2,49,49]{2,3,1,0:T(8,128)(4,1)S(1)}, pred[24,2,49,49]{2,3,1,0:T(8,128)(4,1)}, u32[]{:S(2)}) copy-start(pred[24,2,49,49]{2,3,1,0:T(8,128)(4,1)} %copy-done.6) | copy-start | bytes 345748
  442.9 13.6 %copy-start.8 = (f32[48,16,49]{2,1,0:T(8,128)S(1)}, f32[48,16,49]{2,1,0:T(8,128)}, u32[]{:S(2)}) copy-start(f32[48,16,49]{2,1,0:T(8,128)} %log_add_fusion) | copy-start | bytes 451588
  456.6 63.9 %slice-start = ((s8[6291456]{0:T(1024)(128)(4,1)}), s8[2097152]{0:T(1024)(128)(4,1)S(1)}, s32[]{:S(2)}) async-start(s8[6291456]{0:T(1024)(128)(4,1)} %bitcast.93), calls=%async_computation.13 | async-start | bytes 4194304
  479.9 40.6 %slice-start.1 = ((s8[6291456]{0:T(1024)(128)(4,1)}), s8[4194304]{0:T(1024)(128)(4,1)S(1)}, s32[]{:S(2)}) async-start(s8[6291456]{0:T(1024)(128)(4,1)} %bitcast.93), calls=%async_computation.14 | async-start | bytes 8388608
  542.7 106.8 %reduce-scatter.5.cloned.1.call-start = ((), (), s32[]{:S(2)}) async-start(), calls=%async_computation.7 | async-start | bytes 3932160 | tf_op jit(solution)/shard_map/reduce_scatter | solution.py:285
  604.2 6.0 copy-start.32
  610.1 86.4 %reduce-scatter.11.cloned.1.call-start = ((), (), s32[]{:S(2)}) async-start(), calls=%async_computation.10 | async-start | bytes 5242880 | tf_op jit(solution)/shard_map/reduce_scatter | solution.py:295
  610.2 11.4 %copy-start.28 = (f32[2352]{0:T(1024)S(1)}, f32[2352]{0:T(1024)}, u32[]{:S(2)}) copy-start(f32[2352]{0:T(1024)} %copy-done.27) | copy-start | bytes 28228
  610.2 11.4 %copy-start.30 = (f32[2352]{0:T(1024)S(1)}, f32[2352]{0:T(1024)}, u32[]{:S(2)}) copy-start(f32[2352]{0:T(1024)} %copy-done.29) | copy-start | bytes 28228
  610.2 11.4 %copy-start.39 = (f32[4,1,128]{2,1,0:T(1,128)S(1)}, f32[4,1,128]{2,1,0:T(1,128)}, u32[]{:S(2)}) copy-start(f32[4,1,128]{2,1,0:T(1,128)} %copy-done.38) | copy-start | bytes 6148
  610.2 11.4 %copy-start.47 = (f32[4,1,128]{2,1,0:T(1,128)S(1)}, f32[4,1,128]{2,1,0:T(1,128)}, u32[]{:S(2)}) copy-start(f32[4,1,128]{2,1,0:T(1,128)} %copy-done.46) | copy-start | bytes 6148
  621.3 13.6 %copy-start.22 = (f32[24,7,14]{0,2,1:T(8,128)S(1)}, f32[24,7,14]{0,2,1:T(8,128)}, u32[]{:S(2)}) copy-start(f32[24,7,14]{0,2,1:T(8,128)} %copy-done.21) | copy-start | bytes 28228
  621.3 13.7 %copy-start.19 = (f32[24,7,14]{0,2,1:T(8,128)S(1)}, f32[24,7,14]{0,2,1:T(8,128)}, u32[]{:S(2)}) copy-start(f32[24,7,14]{0,2,1:T(8,128)} %copy-done.18) | copy-start | bytes 28228
  621.3 13.8 %copy-start.58 = (u32[32]{0:T(128)S(1)}, u32[32]{0:T(128)}, u32[]{:S(2)}) copy-start(u32[32]{0:T(128)} %constant.138) | copy-start | bytes 388
  621.3 16.4 %copy-start.54 = (bf16[128]{0:T(256)(128)(2,1)S(1)}, bf16[128]{0:T(256)(128)(2,1)}, u32[]{:S(2)}) copy-start(bf16[128]{0:T(256)(128)(2,1)} %param.33) | copy-start | bytes 772
  621.3 21.8 %copy-start.42 = (f32[24]{0:T(128)S(1)}, f32[24]{0:T(128)}, u32[]{:S(2)}) copy-start(f32[24]{0:T(128)} %copy-done.41) | copy-start | bytes 292
  621.3 122.3 %reduce-scatter.9.cloned.1.call-start = ((), (), s32[]{:S(2)}) async-start(), calls=%async_computation.9 | async-start | bytes 5242880 | tf_op jit(solution)/shard_map/reduce_scatter | solution.py:293
  634.7 8.4 copy-start.14
  634.8 232.6 %all-reduce.18.cloned.1.call-start = ((), (), s32[]{:S(2)}) async-start(), calls=%async_computation.11 | async-start | bytes 6291456 | tf_op jit(solution)/shard_map/psum | solution.py:261
  743.7 211.5 %all-reduce.20.cloned.1.call-start = ((), (), s32[]{:S(2)}) async-start(), calls=%async_computation.12 | async-start | bytes 6291456 | tf_op jit(solution)/shard_map/psum | solution.py:261
  752.9 9.3 slice-start.2
  756.7 5.5 slice-start.3
  760.7 113.6 %collective-permute-start.3 = (bf16[24,3,14,512]{3,0,2,1:T(8,128)(2,1)}, bf16[24,3,14,512]{3,0,2,1:T(8,128)(2,1)}, u32[]{:S(2)}, u32[]{:S(2)}) collective-permute-start(bf16[24,3,14,512]{3,0,2,1:T(8,128)(2,1)} %pad_maximum_fusion.4), channel_id=1, source_target_pairs={{0,16},{16,0},{1,17},{17,1},{2,18},{18,2},{3,19},{19,3},{4,20},{20... | collective-permute-start | bytes 3096584 | tf_op jit(solution)/shard_map/ppermute | solution.py:20
  867.4 6.0 copy-start.36
  867.4 6.9 copy-start.1
  867.4 6.9 copy-start.34
  873.3 6.6 copy-start.37
  873.3 6.6 copy-start.40
  873.3 6.6 copy-start.44
  873.3 6.6 copy-start.45
  955.1 6.1 copy-start.20
  (12 other events, 32.6 us)
Sparse Core Ops, SparseCore 0:
  9.6 22.3 all-gather.13
  33.5 22.6 all-gather.15
  236.7 23.8 all-gather.17
  542.8 26.1 reduce-scatter.6
  610.2 39.2 reduce-scatter.4
  651.9 44.5 reduce-scatter.10
  699.0 44.5 reduce-scatter.8
  746.2 121.0 all-reduce.17
  869.8 85.2 all-reduce.19
